TPU v7x, 32 devices: a whole 2x2x4 slice. The times are simulated.
32 devices in a mesh: pipe: 2 (over x), expert: 16 (over z, y, core).
Axes of the slice: x: 2, y: 2, z: 4, core: 2. Of those that a mesh axis runs over, the one named last changes fastest.
Arguments:
- inputs: bfloat16 [1, 512, 5120], P(None, 'expert'), may hold values from -6 to 6
- router: bfloat16 [2, 5120, 2], P('pipe'), may hold values from -0.078125 to 0.078125
- w_up: bfloat16 [2, 3072, 5120], P('pipe', 'expert'), may hold values from -0.078125 to 0.078125
- w_down: bfloat16 [2, 3072, 5120], P('pipe', 'expert'), may hold values from -0.15625 to 0.15625
- picks: int32 [2, 1, 2, 8], P('pipe'), may hold values from 0 to 511, as said below
- probe: bfloat16 [2, 64, 5120], P('pipe'), may hold values from -0.078125 to 0.078125
Outputs:
- student_feats: bfloat16 [2, 1, 512, 64], P('pipe', None, 'expert')
Inputs may be any that keep to these rules, and one draw needn't show every extreme that they name: Each list picks[s, m, e] holds 8 different token positions of the micro-batch. Of the 32 consecutive positions held by one index of expert, at most 1 stand in one list, and in every list some index has exactly 1.
All inputs are finite; a program needn't handle non-finite values.
Results may differ from a plain program's by a relative error of at most 0.0059.
Values may be sent and summed in bfloat16 or wider, within the bound.
A program may use at most 64 MiB of HBM per device.

v0:
```python
import jax
import jax.numpy as jnp
from jax import lax
from jax.sharding import PartitionSpec as P

SLOT = 1


def passed_along(x, axis, by):
    size = lax.axis_size(axis)
    pairs = [(i, i + by) for i in range(size) if 0 <= i + by < size]
    return lax.ppermute(x, axis, pairs)


def from_root(x, axis, root):
    mine = lax.axis_index(axis) == root
    return lax.psum(jnp.where(mine, x, jnp.zeros_like(x)), axis)


def rms_rows(rows_in):
    wide = rows_in.astype(jnp.float32)
    scale = lax.rsqrt(jnp.mean(wide * wide, axis=-1, keepdims=True) + 1e-06)
    return (wide * scale).astype(jnp.bfloat16)


def shards(inputs, router, w_up, w_down, picks, probe):
    sections = lax.axis_size("pipe")
    expert_width = lax.axis_size("expert")
    section_index = lax.axis_index("pipe")
    source = lax.axis_index("expert")
    micro_count, tok_rows, features = inputs.shape
    experts = router.shape[2]
    group_size = expert_width // experts
    tick_count = micro_count + sections - 1
    positions = jnp.arange(tok_rows, dtype=jnp.int32)
    slot_ids = jnp.arange(SLOT, dtype=jnp.int32)

    def expert_rows(received):
        row_shape = received.shape
        flat_rows = received.reshape(-1, row_shape[2])
        pre = lax.dot_general(
            flat_rows, w_up[0], (((1,), (1,)), ((), ())), preferred_element_type=jnp.float32
        )
        hidden = jax.nn.silu(pre).astype(jnp.bfloat16)
        partials = jnp.dot(hidden, w_down[0], preferred_element_type=jnp.float32).astype(
            jnp.bfloat16
        )
        return partials.reshape(row_shape)

    def layer(rows_in, micro_index):
        normed = rms_rows(rows_in)
        gate_values = jax.nn.sigmoid(jnp.dot(normed, router[0], preferred_element_type=jnp.float32))
        chosen = lax.dynamic_index_in_dim(picks[0], micro_index, 0, keepdims=False)
        local_rows = chosen - source * tok_rows
        owned = (local_rows >= 0) & (local_rows < tok_rows)
        owned_count = owned.astype(jnp.int32)
        slot_place = jnp.cumsum(owned_count, axis=1) - owned_count
        slot_hot = ((slot_place[:, :, None] == slot_ids) & owned[:, :, None]).astype(jnp.bfloat16)
        row_hot = (local_rows[:, :, None] == positions).astype(jnp.bfloat16)
        selector = jnp.einsum("ecr,ect->ert", slot_hot, row_hot, preferred_element_type=jnp.float32)
        picked = jnp.einsum(
            "ert,td->erd", selector.astype(jnp.bfloat16), normed, preferred_element_type=jnp.float32
        ).astype(jnp.bfloat16)
        copies = jnp.repeat(picked, group_size, axis=0)
        partials = expert_rows(
            lax.all_to_all(copies, "expert", split_axis=0, concat_axis=0, tiled=True)
        )
        returned = lax.all_to_all(partials, "expert", split_axis=0, concat_axis=0, tiled=True)
        expert_out = jnp.sum(
            returned.astype(jnp.float32).reshape(experts, group_size, SLOT, features), axis=1
        )
        weights = selector * jnp.transpose(gate_values)[:, None, :]
        update = jnp.einsum("ert,erd->td", weights, expert_out, precision=lax.Precision.HIGHEST)
        return (rows_in.astype(jnp.float32) + update).astype(jnp.bfloat16)

    def tick(tick_index, loop_state):
        previous, finals = loop_state
        arrived = passed_along(previous, "pipe", 1)
        micro_index = jnp.clip(tick_index - section_index, 0, micro_count - 1)
        fresh_rows = lax.dynamic_index_in_dim(
            inputs, jnp.clip(tick_index, 0, micro_count - 1), 0, keepdims=False
        )
        rows_in = jnp.where(section_index == 0, fresh_rows, arrived)
        result = layer(rows_in, micro_index)
        finished = (
            (section_index == sections - 1)
            & (tick_index - section_index >= 0)
            & (tick_index - section_index < micro_count)
        )
        stored = lax.dynamic_update_index_in_dim(finals, result, micro_index, 0)
        finals = jnp.where(finished, stored, finals)
        return (result, finals)

    start_rows = jnp.zeros((tok_rows, features), jnp.bfloat16)
    start_finals = jnp.zeros((micro_count, tok_rows, features), jnp.bfloat16)
    previous, finals = lax.fori_loop(0, tick_count, tick, (start_rows, start_finals))
    shared = from_root(finals, "pipe", sections - 1)
    final_normed = rms_rows(shared)
    student_rows = jnp.einsum(
        "mtd,jd->mtj", final_normed, probe[0], preferred_element_type=jnp.float32
    )
    return student_rows.astype(jnp.bfloat16)[None]


def solution(mesh):
    return jax.shard_map(
        shards,
        mesh=mesh,
        in_specs=(
            P(None, "expert", None),
            P("pipe", None, None),
            P("pipe", "expert", None),
            P("pipe", "expert", None),
            P("pipe", None, None, None),
            P("pipe", None, None),
        ),
        out_specs=P("pipe", None, "expert", None),
        check_vma=False,
    )
```

profile of v0, /device:TPU:0, one launch (start us, length us, event | category | flops | bytes accessed | tf_op | source)
XLA Modules:
  0.0 138.6 jit_solution(14568044816781589299)
XLA Ops:
  6.5 0.0 copy-start
  6.5 0.0 all-reduce.2.cloned.1.call-start
  6.5 0.7 fusion.38
  7.3 0.2 reduce_window_sum.19
  7.5 0.2 fusion.35
  7.7 95.9 %while.21 = (s32[]{:T(128)}, bf16[32,5120]{1,0:T(8,128)(2,1)}, bf16[1,32,5120]{2,1,0:T(8,128)(2,1)}, pred[]{:T(512)}, bf16[1,32,5120]{2,1,0:T(8,128)(2,1)}, /*in...) while((s32[]{:T(128)}, bf16[32,5120]{1,0:T(8,128)(2,1)}, ...), condition=%wide.region_4.5_spmd.clone, body=%wide.region_1.4_spmd.clone.sunk | while | flops 71040296 | bytes 23656336 | solution.py:96
  7.7 0.0 copy-start.1
  7.7 5.0 %collective-permute-start = (bf16[32,5120]{1,0:T(8,128)(2,1)S(1)}, bf16[32,5120]{1,0:T(8,128)(2,1)S(1)}, u32[]{:S(2)}, u32[]{:S(2)}) collective-permute-start(bf16[32,5120]{1,0:T(8,128)(2,1)S(1)} %broadcast_select_fusion.3), channel_id=1, source_target_pairs={{0,16},{1,17},{2,18},{3,19},{4,20},{5,21},{6,22},{7,23},{8,24},{9,... | collective-permute-start | bytes 983048 | tf_op jit(solution)/shard_map/while/body/eval_jaxpr/ppermute | solution.py:12
  12.7 6.9 %collective-permute-done = bf16[32,5120]{1,0:T(8,128)(2,1)S(1)} collective-permute-done((bf16[32,5120]{1,0:T(8,128)(2,1)S(1)}, bf16[32,5120]{1,0:T(8,128)(2,1)S(1)}, u32[]{:S(2)}, u32[]{:S(2)}) %collective-permute-start) | collective-permute-done | bytes 327712 | tf_op jit(solution)/shard_map/while/body/eval_jaxpr/ppermute | solution.py:12
  19.7 1.2 fusion.64
  20.9 0.2 fusion.65
  21.2 0.6 broadcast.199
  21.8 0.8 reduce.13
  22.5 0.1 reshape.138
  22.6 14.2 %all_to_all.32 = bf16[16,2,2560]{2,1,0:T(2,128)(2,1)S(1)} all-to-all(bf16[16,2,2560]{2,1,0:T(2,128)(2,1)S(1)} %reshape.138), channel_id=1, replica_groups=mesh['pipe'=2,'expert'=16] {'expert'}, dimensions={0} | all-to-all | bytes 327680 | tf_op jit(solution)/shard_map/while/body/eval_jaxpr/all_to_all | solution.py:66
  36.8 0.1 reshape.139
  36.9 0.0 copy-done.1
  36.9 0.0 copy-start.4
  37.0 3.0 %fusion.66 = bf16[16,1,5120]{2,0,1:T(8,128)(2,1)S(1)} fusion(bf16[1,192,5120]{2,1,0:T(8,128)(2,1)} %get-tuple-element.587, bf16[1,192,5120]{2,1,0:T(8,128)(2,1)S(1)} %copy-done.1, bf16[16,1,5120]{2,1,0:T(2,128)(2,1)S(1)} %reshape.139), kind=kOutput, calls=%fused_computation.3.clone.1 | convolution fusion | flops 63011840 | bytes 4259840 | tf_op jit(solution)/shard_map/while/body/eval_jaxpr/dot_general | solution.py:45
  40.0 0.6 broadcast.200
  40.6 0.8 reduce.14
  41.4 0.8 reshape.140
  42.1 3.5 %all-to-all-start.1 = ((bf16[16,2,2560]{2,1,0:T(2,128)(2,1)}), bf16[16,2,2560]{2,1,0:T(2,128)(2,1)S(1)}, u32[]{:S(2)}, u32[]{:S(2)}) async-start(bf16[16,2,2560]{2,1,0:T(2,128)(2,1)} %reshape.140), calls=%async_computation.1 | async-start | bytes 327680 | tf_op jit(solution)/shard_map/while/body/eval_jaxpr/all_to_all | solution.py:68
  45.7 0.0 copy-done.4
  45.7 0.3 fusion.67
  45.9 8.1 %all-to-all-done.1 = bf16[16,2,2560]{2,1,0:T(2,128)(2,1)S(1)} async-done(((bf16[16,2,2560]{2,1,0:T(2,128)(2,1)}), bf16[16,2,2560]{2,1,0:T(2,128)(2,1)S(1)}, u32[]{:S(2)}, u32[]{:S(2)}) %all-to-all-start.1) | async-done | bytes 163872 | tf_op jit(solution)/shard_map/while/body/eval_jaxpr/all_to_all | solution.py:68
  54.0 0.1 reshape.141
  54.2 0.3 reshape.142
  54.5 0.1 bitcast_reduce_fusion.2
  54.7 0.0 copy-done.2
  54.7 1.6 %bitcast_select_fusion.4 = (bf16[1,32,5120]{2,1,0:T(8,128)(2,1)S(1)}, bf16[32,5120]{1,0:T(8,128)(2,1)}) fusion(bf16[1,32,5120]{2,1,0:T(8,128)(2,1)S(1)} %copy-done.2, pred[]{:T(512)S(6)} %compare.3, pred[]{:T(512)S(6)} %and.69, f32[2,32]{1,0:T(2,128)S(1)} %fusion.67, f32[2,5120]{1,0:T(2,128)S(1)} %bitcast_reduce_fusion.2, ...), kind=kOutput, calls=%fused_computation.20.clone.1 | convolution fusion | flops 4751360 | bytes 1351938 | tf_op jit(solution)/shard_map/while/body/eval_jaxpr/ert,erd->td/dot_general | solution.py:73
  56.2 0.7 copy-done.3
  57.0 1.1 broadcast_select_fusion.3
  58.1 4.4 %collective-permute-start = (bf16[32,5120]{1,0:T(8,128)(2,1)S(1)}, bf16[32,5120]{1,0:T(8,128)(2,1)S(1)}, u32[]{:S(2)}, u32[]{:S(2)}) collective-permute-start(bf16[32,5120]{1,0:T(8,128)(2,1)S(1)} %broadcast_select_fusion.3), channel_id=1, source_target_pairs={{0,16},{1,17},{2,18},{3,19},{4,20},{5,21},{6,22},{7,23},{8,24},{9,... | collective-permute-start | bytes 983048 | tf_op jit(solution)/shard_map/while/body/eval_jaxpr/ppermute | solution.py:12
  62.5 6.3 %collective-permute-done = bf16[32,5120]{1,0:T(8,128)(2,1)S(1)} collective-permute-done((bf16[32,5120]{1,0:T(8,128)(2,1)S(1)}, bf16[32,5120]{1,0:T(8,128)(2,1)S(1)}, u32[]{:S(2)}, u32[]{:S(2)}) %collective-permute-start) | collective-permute-done | bytes 327712 | tf_op jit(solution)/shard_map/while/body/eval_jaxpr/ppermute | solution.py:12
  68.9 1.2 fusion.64
  70.1 0.2 fusion.65
  70.4 0.6 broadcast.199
  71.0 0.8 reduce.13
  71.7 0.1 reshape.138
  71.8 11.6 %all_to_all.32 = bf16[16,2,2560]{2,1,0:T(2,128)(2,1)S(1)} all-to-all(bf16[16,2,2560]{2,1,0:T(2,128)(2,1)S(1)} %reshape.138), channel_id=1, replica_groups=mesh['pipe'=2,'expert'=16] {'expert'}, dimensions={0} | all-to-all | bytes 327680 | tf_op jit(solution)/shard_map/while/body/eval_jaxpr/all_to_all | solution.py:66
  83.4 0.1 reshape.139
  83.6 0.0 copy-done.1
  83.6 0.0 copy-start.4
  83.6 3.0 %fusion.66 = bf16[16,1,5120]{2,0,1:T(8,128)(2,1)S(1)} fusion(bf16[1,192,5120]{2,1,0:T(8,128)(2,1)} %get-tuple-element.587, bf16[1,192,5120]{2,1,0:T(8,128)(2,1)S(1)} %copy-done.1, bf16[16,1,5120]{2,1,0:T(2,128)(2,1)S(1)} %reshape.139), kind=kOutput, calls=%fused_computation.3.clone.1 | convolution fusion | flops 63011840 | bytes 4259840 | tf_op jit(solution)/shard_map/while/body/eval_jaxpr/dot_general | solution.py:45
  86.6 0.6 broadcast.200
  87.2 0.8 reduce.14
  88.0 0.8 reshape.140
  88.7 3.5 %all-to-all-start.1 = ((bf16[16,2,2560]{2,1,0:T(2,128)(2,1)}), bf16[16,2,2560]{2,1,0:T(2,128)(2,1)S(1)}, u32[]{:S(2)}, u32[]{:S(2)}) async-start(bf16[16,2,2560]{2,1,0:T(2,128)(2,1)} %reshape.140), calls=%async_computation.1 | async-start | bytes 327680 | tf_op jit(solution)/shard_map/while/body/eval_jaxpr/all_to_all | solution.py:68
  92.3 0.0 copy-done.4
  92.3 0.3 fusion.67
  92.6 8.1 %all-to-all-done.1 = bf16[16,2,2560]{2,1,0:T(2,128)(2,1)S(1)} async-done(((bf16[16,2,2560]{2,1,0:T(2,128)(2,1)}), bf16[16,2,2560]{2,1,0:T(2,128)(2,1)S(1)}, u32[]{:S(2)}, u32[]{:S(2)}) %all-to-all-start.1) | async-done | bytes 163872 | tf_op jit(solution)/shard_map/while/body/eval_jaxpr/all_to_all | solution.py:68
  100.7 0.1 reshape.141
  100.8 0.3 reshape.142
  101.1 0.1 bitcast_reduce_fusion.2
  101.3 0.0 copy-done.2
  101.3 1.6 %bitcast_select_fusion.4 = (bf16[1,32,5120]{2,1,0:T(8,128)(2,1)S(1)}, bf16[32,5120]{1,0:T(8,128)(2,1)}) fusion(bf16[1,32,5120]{2,1,0:T(8,128)(2,1)S(1)} %copy-done.2, pred[]{:T(512)S(6)} %compare.3, pred[]{:T(512)S(6)} %and.69, f32[2,32]{1,0:T(2,128)S(1)} %fusion.67, f32[2,5120]{1,0:T(2,128)S(1)} %bitcast_reduce_fusion.2, ...), kind=kOutput, calls=%fused_computation.20.clone.1 | convolution fusion | flops 4751360 | bytes 1351938 | tf_op jit(solution)/shard_map/while/body/eval_jaxpr/ert,erd->td/dot_general | solution.py:73
  102.9 0.7 copy-done.3
  103.6 0.7 broadcast_select_fusion.1
  104.3 0.0 all-reduce.2.cloned.1.call-update
  104.4 24.3 %all-reduce.2.cloned.1.call-done = bf16[1,32,5120]{2,1,0:T(8,128)(2,1)} async-done(((bf16[1,32,5120]{2,1,0:T(8,128)(2,1)}), bf16[1,32,5120]{2,1,0:T(8,128)(2,1)}) %all-reduce.2.cloned.1.call-update) | async-done | bytes 327696 | tf_op jit(solution)/shard_map/psum | solution.py:17
  128.6 1.1 fusion.29
  129.8 0.0 copy-done
  129.8 1.9 %fusion.28 = bf16[1,1,32,64]{3,2,1,0:T(8,128)(2,1)} fusion(bf16[1,64,5120]{2,1,0:T(8,128)(2,1)S(1)} %copy-done, bf16[1,32,5120]{2,1,0:T(8,128)(2,1)} %all-reduce.2.cloned.1.call-done, f32[32]{0:T(128)S(1)} %add_rsqrt_fusion.1), kind=kOutput, calls=%fused_computation.32 | convolution fusion | flops 21465088 | bytes 987264 | tf_op jit(solution)/shard_map/mtd,jd->mtj/dot_general | solution.py:99
  (15 shorter events, 0.1 us)
Async XLA Ops:
  6.5 123.3 %copy-start = (bf16[1,64,5120]{2,1,0:T(8,128)(2,1)S(1)}, bf16[1,64,5120]{2,1,0:T(8,128)(2,1)}, u32[]{:S(2)}) copy-start(bf16[1,64,5120]{2,1,0:T(8,128)(2,1)} %param.13) | copy-start | bytes 1966084
  6.5 122.1 %all-reduce.2.cloned.1.call-start = ((), (), s32[]{:S(2)}) async-start(), calls=%async_computation.2 | async-start | bytes 655360 | tf_op jit(solution)/shard_map/psum | solution.py:17
  7.7 29.3 %copy-start.1 = (bf16[1,192,5120]{2,1,0:T(8,128)(2,1)S(1)}, bf16[1,192,5120]{2,1,0:T(8,128)(2,1)}, u32[]{:S(2)}) copy-start(bf16[1,192,5120]{2,1,0:T(8,128)(2,1)} %get-tuple-element.586) | copy-start | bytes 5898244 | tf_op jit(solution)/shard_map/while
  7.7 12.0 %collective-permute-start = (bf16[32,5120]{1,0:T(8,128)(2,1)S(1)}, bf16[32,5120]{1,0:T(8,128)(2,1)S(1)}, u32[]{:S(2)}, u32[]{:S(2)}) collective-permute-start(bf16[32,5120]{1,0:T(8,128)(2,1)S(1)} %broadcast_select_fusion.3), channel_id=1, source_target_pairs={{0,16},{1,17},{2,18},{3,19},{4,20},{5,21},{6,22},{7,23},{8,24},{9,... | collective-permute-start | bytes 983048 | tf_op jit(solution)/shard_map/while/body/eval_jaxpr/ppermute | solution.py:12
  36.9 8.7 %copy-start.4 = (bf16[1,5120,2]{1,2,0:T(2,128)(2,1)S(1)}, bf16[1,5120,2]{1,2,0:T(2,128)(2,1)}, u32[]{:S(2)}) copy-start(bf16[1,5120,2]{1,2,0:T(2,128)(2,1)} %get-tuple-element.583) | copy-start | bytes 61444 | tf_op jit(solution)/shard_map/while
  40.0 14.7 %copy-start.2 = (bf16[1,32,5120]{2,1,0:T(8,128)(2,1)S(1)}, bf16[1,32,5120]{2,1,0:T(8,128)(2,1)}, u32[]{:S(2)}) copy-start(bf16[1,32,5120]{2,1,0:T(8,128)(2,1)} %get-tuple-element.564) | copy-start | bytes 983044 | tf_op jit(solution)/shard_map/while
  42.1 11.9 %all-to-all-start.1 = ((bf16[16,2,2560]{2,1,0:T(2,128)(2,1)}), bf16[16,2,2560]{2,1,0:T(2,128)(2,1)S(1)}, u32[]{:S(2)}, u32[]{:S(2)}) async-start(bf16[16,2,2560]{2,1,0:T(2,128)(2,1)} %reshape.140), calls=%async_computation.1 | async-start | bytes 327680 | tf_op jit(solution)/shard_map/while/body/eval_jaxpr/all_to_all | solution.py:68
  56.2 0.7 copy-start.3
  57.0 26.6 %copy-start.1 = (bf16[1,192,5120]{2,1,0:T(8,128)(2,1)S(1)}, bf16[1,192,5120]{2,1,0:T(8,128)(2,1)}, u32[]{:S(2)}) copy-start(bf16[1,192,5120]{2,1,0:T(8,128)(2,1)} %get-tuple-element.586) | copy-start | bytes 5898244 | tf_op jit(solution)/shard_map/while
  58.1 10.8 %collective-permute-start = (bf16[32,5120]{1,0:T(8,128)(2,1)S(1)}, bf16[32,5120]{1,0:T(8,128)(2,1)S(1)}, u32[]{:S(2)}, u32[]{:S(2)}) collective-permute-start(bf16[32,5120]{1,0:T(8,128)(2,1)S(1)} %broadcast_select_fusion.3), channel_id=1, source_target_pairs={{0,16},{1,17},{2,18},{3,19},{4,20},{5,21},{6,22},{7,23},{8,24},{9,... | collective-permute-start | bytes 983048 | tf_op jit(solution)/shard_map/while/body/eval_jaxpr/ppermute | solution.py:12
  83.6 8.7 %copy-start.4 = (bf16[1,5120,2]{1,2,0:T(2,128)(2,1)S(1)}, bf16[1,5120,2]{1,2,0:T(2,128)(2,1)}, u32[]{:S(2)}) copy-start(bf16[1,5120,2]{1,2,0:T(2,128)(2,1)} %get-tuple-element.583) | copy-start | bytes 61444 | tf_op jit(solution)/shard_map/while
  86.6 14.7 %copy-start.2 = (bf16[1,32,5120]{2,1,0:T(8,128)(2,1)S(1)}, bf16[1,32,5120]{2,1,0:T(8,128)(2,1)}, u32[]{:S(2)}) copy-start(bf16[1,32,5120]{2,1,0:T(8,128)(2,1)} %get-tuple-element.564) | copy-start | bytes 983044 | tf_op jit(solution)/shard_map/while
  88.7 11.9 %all-to-all-start.1 = ((bf16[16,2,2560]{2,1,0:T(2,128)(2,1)}), bf16[16,2,2560]{2,1,0:T(2,128)(2,1)S(1)}, u32[]{:S(2)}, u32[]{:S(2)}) async-start(bf16[16,2,2560]{2,1,0:T(2,128)(2,1)} %reshape.140), calls=%async_computation.1 | async-start | bytes 327680 | tf_op jit(solution)/shard_map/while/body/eval_jaxpr/all_to_all | solution.py:68
  102.9 0.7 copy-start.3
Sparse Core Ops, SparseCore 0:
  104.5 24.1 all-reduce.1
where the time goes:
time: 139 us
  waiting for transfers between devices  53.8 us (39%)
  blocking collectives  25.8 us (19%)
  starting transfers between devices  16.5 us (12%)
  between operations  13.4 us (10%)
  matrix products  12.4 us (9%)
  other arithmetic  10.4 us (7%)
  local copies, waits for them, and re-layouts  6.15 us (4%)
    all_to_all x2, blocking collectives, layer(): lax.all_to_all(copies, 'expert', split_axis=0, concat_axis=0, tiled=True)  25.8 us
    psum x1, waiting for transfers between devices, from_root(): return lax.psum(jnp.where(mine, x, jnp.zeros_like(x)), axis)  24.3 us
    all_to_all x2, waiting for transfers between devices, layer(): lax.all_to_all(partials, 'expert', split_axis=0, concat_axis=0, tiled=True)  16.2 us
    ppermute x2, waiting for transfers between devices, passed_along(): return lax.ppermute(x, axis, pairs)  13.3 us
    ppermute x2, starting transfers between devices, passed_along(): return lax.ppermute(x, axis, pairs)  9.43 us
    all_to_all x2, starting transfers between devices, layer(): lax.all_to_all(partials, 'expert', split_axis=0, concat_axis=0, tiled=True)  7.03 us
    dot_general x2, matrix products, expert_rows(): jnp.dot(hidden, w_down[0], preferred_element_type=jnp.float32)  6.05 us
    while x24, local copies, waits for them, and re-layouts  3.7 us
  transfers between devices with their start and end apart: 5, of which 5 were waited for; matrix products, arithmetic and copies ran while one was open for 0% of the time, Pallas kernels for 0%

commit v1 on v0

--- a/solution.py
+++ b/solution.py
@@ -14,7 +14,7 @@
 
 def from_root(x, axis, root):
     mine = lax.axis_index(axis) == root
-    return lax.psum(jnp.where(mine, x, jnp.zeros_like(x)), axis)
+    return jnp.sum(lax.all_gather(jnp.where(mine, x, jnp.zeros_like(x)), axis), axis=0)
 
 
 def rms_rows(rows_in):

time: 139 us -> 110 us (0.79)
  waiting for transfers between devices: 53.8 us -> 29.5 us
  between operations: 13.4 us -> 0.02 us
  blocking collectives: 25.8 us -> 37 us
    psum x1 -> x0, waiting for transfers between devices: 24.3 us -> none  [from_root(): return lax.psum(jnp.where(mine, x, jnp.zeros_like(x)), axis)]
    all_gather x0 -> x1, blocking collectives: none -> 11.2 us  [from_root(): lax.all_gather(jnp.where(mine, x, jnp.zeros_like(x)), axis)]
  transfers between devices with their start and end apart: 5 -> 4, of which waited for: 5 -> 4; matrix products, arithmetic and copies ran while one was open for 0% -> 1% of each run, Pallas kernels for 0% -> 0%
where the time goes in v1:
time: 110 us
  blocking collectives  37 us (34%)
  waiting for transfers between devices  29.5 us (27%)
  starting transfers between devices  16.5 us (15%)
  matrix products  11.4 us (10%)
  other arithmetic  9.03 us (8%)
  local copies, waits for them, and re-layouts  6.15 us (6%)
    all_to_all x2, blocking collectives, layer(): lax.all_to_all(copies, 'expert', split_axis=0, concat_axis=0, tiled=True)  25.8 us
    all_to_all x2, waiting for transfers between devices, layer(): lax.all_to_all(partials, 'expert', split_axis=0, concat_axis=0, tiled=True)  16.2 us
    ppermute x2, waiting for transfers between devices, passed_along(): return lax.ppermute(x, axis, pairs)  13.3 us
    all_gather x1, blocking collectives, from_root(): lax.all_gather(jnp.where(mine, x, jnp.zeros_like(x)), axis)  11.2 us
    ppermute x2, starting transfers between devices, passed_along(): return lax.ppermute(x, axis, pairs)  9.43 us
    all_to_all x2, starting transfers between devices, layer(): lax.all_to_all(partials, 'expert', split_axis=0, concat_axis=0, tiled=True)  7.03 us
    dot_general x2, matrix products, expert_rows(): jnp.dot(hidden, w_down[0], preferred_element_type=jnp.float32)  6.05 us
    while x24, local copies, waits for them, and re-layouts  3.7 us
  transfers between devices with their start and end apart: 4, of which 4 were waited for; matrix products, arithmetic and copies ran while one was open for 1% of the time, Pallas kernels for 0%

profile of v1, /device:TPU:0, one launch (start us, length us, event | category | flops | bytes accessed | tf_op | source)
XLA Modules:
  0.0 109.8 jit_solution(3518336086595866970)
XLA Ops:
  0.0 0.0 copy-start
  0.0 0.7 fusion.39
  0.8 0.2 reduce_window_sum.19
  0.9 0.2 fusion.36
  1.1 95.9 %while.21 = (s32[]{:T(128)}, bf16[32,5120]{1,0:T(8,128)(2,1)}, bf16[1,32,5120]{2,1,0:T(8,128)(2,1)}, pred[]{:T(512)}, bf16[1,32,5120]{2,1,0:T(8,128)(2,1)}, /*in...) while((s32[]{:T(128)}, bf16[32,5120]{1,0:T(8,128)(2,1)}, ...), condition=%wide.region_4.5_spmd.clone, body=%wide.region_1.4_spmd.clone.sunk | while | flops 71040296 | bytes 23656336 | solution.py:96
  1.1 0.0 copy-start.1
  1.2 5.0 %collective-permute-start = (bf16[32,5120]{1,0:T(8,128)(2,1)S(1)}, bf16[32,5120]{1,0:T(8,128)(2,1)S(1)}, u32[]{:S(2)}, u32[]{:S(2)}) collective-permute-start(bf16[32,5120]{1,0:T(8,128)(2,1)S(1)} %broadcast_select_fusion.3), channel_id=1, source_target_pairs={{0,16},{1,17},{2,18},{3,19},{4,20},{5,21},{6,22},{7,23},{8,24},{9,... | collective-permute-start | bytes 983048 | tf_op jit(solution)/shard_map/while/body/eval_jaxpr/ppermute | solution.py:12
  6.2 6.9 %collective-permute-done = bf16[32,5120]{1,0:T(8,128)(2,1)S(1)} collective-permute-done((bf16[32,5120]{1,0:T(8,128)(2,1)S(1)}, bf16[32,5120]{1,0:T(8,128)(2,1)S(1)}, u32[]{:S(2)}, u32[]{:S(2)}) %collective-permute-start) | collective-permute-done | bytes 327712 | tf_op jit(solution)/shard_map/while/body/eval_jaxpr/ppermute | solution.py:12
  13.2 1.2 %fusion.65 = (f32[32]{0:T(128)S(1)}, bf16[32,5120]{1,0:T(8,128)(2,1)S(1)}) fusion(bf16[32,5120]{1,0:T(8,128)(2,1)S(1)} %collective-permute-done, bf16[1,32,5120]{2,1,0:T(8,128)(2,1)} %get-tuple-element.582, pred[]{:T(512)} %get-tuple-element.581), kind=kLoop, calls=%fused_computation.17.clone.1 | loop fusion | flops 655328 | bytes 983169 | tf_op jit(solution)/shard_map/while/body/eval_jaxpr/reduce_sum | solution.py:22
  14.4 0.2 fusion.66
  14.7 0.6 broadcast.216
  15.3 0.8 reduce.18
  16.0 0.1 reshape.189
  16.1 14.2 %all_to_all.32 = bf16[16,2,2560]{2,1,0:T(2,128)(2,1)S(1)} all-to-all(bf16[16,2,2560]{2,1,0:T(2,128)(2,1)S(1)} %reshape.189), channel_id=1, replica_groups=mesh['pipe'=2,'expert'=16] {'expert'}, dimensions={0} | all-to-all | bytes 327680 | tf_op jit(solution)/shard_map/while/body/eval_jaxpr/all_to_all | solution.py:66
  30.3 0.1 reshape.190
  30.4 0.0 copy-done.1
  30.4 0.0 copy-start.4
  30.4 3.0 %fusion.67 = bf16[16,1,5120]{2,0,1:T(8,128)(2,1)S(1)} fusion(bf16[1,192,5120]{2,1,0:T(8,128)(2,1)} %get-tuple-element.587, bf16[1,192,5120]{2,1,0:T(8,128)(2,1)S(1)} %copy-done.1, bf16[16,1,5120]{2,1,0:T(2,128)(2,1)S(1)} %reshape.190), kind=kOutput, calls=%fused_computation.3.clone.1 | convolution fusion | flops 63011840 | bytes 4259840 | tf_op jit(solution)/shard_map/while/body/eval_jaxpr/dot_general | solution.py:45
  33.5 0.0 copy-start.2
  33.5 0.6 broadcast.217
  34.1 0.8 reduce.19
  34.8 0.8 reshape.191
  35.6 3.5 %all-to-all-start.1 = ((bf16[16,2,2560]{2,1,0:T(2,128)(2,1)}), bf16[16,2,2560]{2,1,0:T(2,128)(2,1)S(1)}, u32[]{:S(2)}, u32[]{:S(2)}) async-start(bf16[16,2,2560]{2,1,0:T(2,128)(2,1)} %reshape.191), calls=%async_computation.1 | async-start | bytes 327680 | tf_op jit(solution)/shard_map/while/body/eval_jaxpr/all_to_all | solution.py:68
  39.1 0.0 copy-done.4
  39.1 0.3 fusion.68
  39.4 8.1 %all-to-all-done.1 = bf16[16,2,2560]{2,1,0:T(2,128)(2,1)S(1)} async-done(((bf16[16,2,2560]{2,1,0:T(2,128)(2,1)}), bf16[16,2,2560]{2,1,0:T(2,128)(2,1)S(1)}, u32[]{:S(2)}, u32[]{:S(2)}) %all-to-all-start.1) | async-done | bytes 163872 | tf_op jit(solution)/shard_map/while/body/eval_jaxpr/all_to_all | solution.py:68
  47.5 0.1 reshape.192
  47.6 0.3 reshape.193
  48.0 0.1 bitcast_reduce_fusion.2
  48.1 0.0 copy-done.2
  48.1 1.6 %bitcast_select_fusion.4 = (bf16[1,32,5120]{2,1,0:T(8,128)(2,1)S(1)}, bf16[32,5120]{1,0:T(8,128)(2,1)}) fusion(bf16[1,32,5120]{2,1,0:T(8,128)(2,1)S(1)} %copy-done.2, pred[]{:T(512)S(6)} %compare.3, pred[]{:T(512)S(6)} %and.69, f32[2,32]{1,0:T(2,128)S(1)} %fusion.68, f32[2,5120]{1,0:T(2,128)S(1)} %bitcast_reduce_fusion.2, ...), kind=kOutput, calls=%fused_computation.20.clone.1 | convolution fusion | flops 4751360 | bytes 1351938 | tf_op jit(solution)/shard_map/while/body/eval_jaxpr/ert,erd->td/dot_general | solution.py:73
  49.7 0.0 copy-start.3
  49.7 0.7 copy-done.3
  50.5 1.1 %broadcast_select_fusion.3 = bf16[32,5120]{1,0:T(8,128)(2,1)S(1)} fusion(bf16[32,5120]{1,0:T(8,128)(2,1)} %get-tuple-element.563, pred[]{:T(512)S(6)} %compare.3), kind=kLoop, calls=%fused_computation.22.clone.1 | loop fusion | flops 163840 | bytes 655361 | tf_op jit(solution)/shard_map/while
  51.6 4.4 %collective-permute-start = (bf16[32,5120]{1,0:T(8,128)(2,1)S(1)}, bf16[32,5120]{1,0:T(8,128)(2,1)S(1)}, u32[]{:S(2)}, u32[]{:S(2)}) collective-permute-start(bf16[32,5120]{1,0:T(8,128)(2,1)S(1)} %broadcast_select_fusion.3), channel_id=1, source_target_pairs={{0,16},{1,17},{2,18},{3,19},{4,20},{5,21},{6,22},{7,23},{8,24},{9,... | collective-permute-start | bytes 983048 | tf_op jit(solution)/shard_map/while/body/eval_jaxpr/ppermute | solution.py:12
  56.0 6.3 %collective-permute-done = bf16[32,5120]{1,0:T(8,128)(2,1)S(1)} collective-permute-done((bf16[32,5120]{1,0:T(8,128)(2,1)S(1)}, bf16[32,5120]{1,0:T(8,128)(2,1)S(1)}, u32[]{:S(2)}, u32[]{:S(2)}) %collective-permute-start) | collective-permute-done | bytes 327712 | tf_op jit(solution)/shard_map/while/body/eval_jaxpr/ppermute | solution.py:12
  62.4 1.2 %fusion.65 = (f32[32]{0:T(128)S(1)}, bf16[32,5120]{1,0:T(8,128)(2,1)S(1)}) fusion(bf16[32,5120]{1,0:T(8,128)(2,1)S(1)} %collective-permute-done, bf16[1,32,5120]{2,1,0:T(8,128)(2,1)} %get-tuple-element.582, pred[]{:T(512)} %get-tuple-element.581), kind=kLoop, calls=%fused_computation.17.clone.1 | loop fusion | flops 655328 | bytes 983169 | tf_op jit(solution)/shard_map/while/body/eval_jaxpr/reduce_sum | solution.py:22
  63.6 0.2 fusion.66
  63.9 0.6 broadcast.216
  64.4 0.8 reduce.18
  65.2 0.1 reshape.189
  65.3 11.6 %all_to_all.32 = bf16[16,2,2560]{2,1,0:T(2,128)(2,1)S(1)} all-to-all(bf16[16,2,2560]{2,1,0:T(2,128)(2,1)S(1)} %reshape.189), channel_id=1, replica_groups=mesh['pipe'=2,'expert'=16] {'expert'}, dimensions={0} | all-to-all | bytes 327680 | tf_op jit(solution)/shard_map/while/body/eval_jaxpr/all_to_all | solution.py:66
  76.9 0.1 reshape.190
  77.0 0.0 copy-done.1
  77.1 0.0 copy-start.4
  77.1 3.0 %fusion.67 = bf16[16,1,5120]{2,0,1:T(8,128)(2,1)S(1)} fusion(bf16[1,192,5120]{2,1,0:T(8,128)(2,1)} %get-tuple-element.587, bf16[1,192,5120]{2,1,0:T(8,128)(2,1)S(1)} %copy-done.1, bf16[16,1,5120]{2,1,0:T(2,128)(2,1)S(1)} %reshape.190), kind=kOutput, calls=%fused_computation.3.clone.1 | convolution fusion | flops 63011840 | bytes 4259840 | tf_op jit(solution)/shard_map/while/body/eval_jaxpr/dot_general | solution.py:45
  80.1 0.6 broadcast.217
  80.7 0.8 reduce.19
  81.5 0.8 reshape.191
  82.2 3.5 %all-to-all-start.1 = ((bf16[16,2,2560]{2,1,0:T(2,128)(2,1)}), bf16[16,2,2560]{2,1,0:T(2,128)(2,1)S(1)}, u32[]{:S(2)}, u32[]{:S(2)}) async-start(bf16[16,2,2560]{2,1,0:T(2,128)(2,1)} %reshape.191), calls=%async_computation.1 | async-start | bytes 327680 | tf_op jit(solution)/shard_map/while/body/eval_jaxpr/all_to_all | solution.py:68
  85.8 0.0 copy-done.4
  85.8 0.3 fusion.68
  86.0 8.1 %all-to-all-done.1 = bf16[16,2,2560]{2,1,0:T(2,128)(2,1)S(1)} async-done(((bf16[16,2,2560]{2,1,0:T(2,128)(2,1)}), bf16[16,2,2560]{2,1,0:T(2,128)(2,1)S(1)}, u32[]{:S(2)}, u32[]{:S(2)}) %all-to-all-start.1) | async-done | bytes 163872 | tf_op jit(solution)/shard_map/while/body/eval_jaxpr/all_to_all | solution.py:68
  94.1 0.1 reshape.192
  94.3 0.3 reshape.193
  94.6 0.1 bitcast_reduce_fusion.2
  94.8 0.0 copy-done.2
  94.8 1.6 %bitcast_select_fusion.4 = (bf16[1,32,5120]{2,1,0:T(8,128)(2,1)S(1)}, bf16[32,5120]{1,0:T(8,128)(2,1)}) fusion(bf16[1,32,5120]{2,1,0:T(8,128)(2,1)S(1)} %copy-done.2, pred[]{:T(512)S(6)} %compare.3, pred[]{:T(512)S(6)} %and.69, f32[2,32]{1,0:T(2,128)S(1)} %fusion.68, f32[2,5120]{1,0:T(2,128)S(1)} %bitcast_reduce_fusion.2, ...), kind=kOutput, calls=%fused_computation.20.clone.1 | convolution fusion | flops 4751360 | bytes 1351938 | tf_op jit(solution)/shard_map/while/body/eval_jaxpr/ert,erd->td/dot_general | solution.py:73
  96.4 0.7 copy-done.3
  97.1 11.2 %all-gather = bf16[2,32,5120]{2,1,0:T(8,128)(2,1)S(1)} all-gather(bf16[1,32,5120]{2,1,0:T(8,128)(2,1)S(1)} %broadcast_select_fusion.1), channel_id=2, replica_groups=mesh['pipe'=2,'expert'=16] {'pipe'}, dimensions={0}, use_global_device_ids=true | all-gather | bytes 983040 | tf_op jit(solution)/shard_map/all_gather | solution.py:17
  108.4 0.2 reduce.12
  108.6 0.2 fusion.31
  108.8 0.0 copy-done
  108.8 1.0 fusion.28
  (14 shorter events, 0.2 us)
Async XLA Ops:
  0.0 108.8 %copy-start = (bf16[1,64,5120]{2,1,0:T(8,128)(2,1)S(1)}, bf16[1,64,5120]{2,1,0:T(8,128)(2,1)}, u32[]{:S(2)}) copy-start(bf16[1,64,5120]{2,1,0:T(8,128)(2,1)} %param.13) | copy-start | bytes 1966084
  1.1 29.3 %copy-start.1 = (bf16[1,192,5120]{2,1,0:T(8,128)(2,1)S(1)}, bf16[1,192,5120]{2,1,0:T(8,128)(2,1)}, u32[]{:S(2)}) copy-start(bf16[1,192,5120]{2,1,0:T(8,128)(2,1)} %get-tuple-element.586) | copy-start | bytes 5898244 | tf_op jit(solution)/shard_map/while
  1.2 12.0 %collective-permute-start = (bf16[32,5120]{1,0:T(8,128)(2,1)S(1)}, bf16[32,5120]{1,0:T(8,128)(2,1)S(1)}, u32[]{:S(2)}, u32[]{:S(2)}) collective-permute-start(bf16[32,5120]{1,0:T(8,128)(2,1)S(1)} %broadcast_select_fusion.3), channel_id=1, source_target_pairs={{0,16},{1,17},{2,18},{3,19},{4,20},{5,21},{6,22},{7,23},{8,24},{9,... | collective-permute-start | bytes 983048 | tf_op jit(solution)/shard_map/while/body/eval_jaxpr/ppermute | solution.py:12
  30.4 8.7 %copy-start.4 = (bf16[1,5120,2]{1,2,0:T(2,128)(2,1)S(1)}, bf16[1,5120,2]{1,2,0:T(2,128)(2,1)}, u32[]{:S(2)}) copy-start(bf16[1,5120,2]{1,2,0:T(2,128)(2,1)} %get-tuple-element.583) | copy-start | bytes 61444 | tf_op jit(solution)/shard_map/while
  33.5 14.7 %copy-start.2 = (bf16[1,32,5120]{2,1,0:T(8,128)(2,1)S(1)}, bf16[1,32,5120]{2,1,0:T(8,128)(2,1)}, u32[]{:S(2)}) copy-start(bf16[1,32,5120]{2,1,0:T(8,128)(2,1)} %get-tuple-element.564) | copy-start | bytes 983044 | tf_op jit(solution)/shard_map/while
  35.6 11.9 %all-to-all-start.1 = ((bf16[16,2,2560]{2,1,0:T(2,128)(2,1)}), bf16[16,2,2560]{2,1,0:T(2,128)(2,1)S(1)}, u32[]{:S(2)}, u32[]{:S(2)}) async-start(bf16[16,2,2560]{2,1,0:T(2,128)(2,1)} %reshape.191), calls=%async_computation.1 | async-start | bytes 327680 | tf_op jit(solution)/shard_map/while/body/eval_jaxpr/all_to_all | solution.py:68
  49.7 0.7 copy-start.3
  50.4 26.6 %copy-start.1 = (bf16[1,192,5120]{2,1,0:T(8,128)(2,1)S(1)}, bf16[1,192,5120]{2,1,0:T(8,128)(2,1)}, u32[]{:S(2)}) copy-start(bf16[1,192,5120]{2,1,0:T(8,128)(2,1)} %get-tuple-element.586) | copy-start | bytes 5898244 | tf_op jit(solution)/shard_map/while
  51.6 10.8 %collective-permute-start = (bf16[32,5120]{1,0:T(8,128)(2,1)S(1)}, bf16[32,5120]{1,0:T(8,128)(2,1)S(1)}, u32[]{:S(2)}, u32[]{:S(2)}) collective-permute-start(bf16[32,5120]{1,0:T(8,128)(2,1)S(1)} %broadcast_select_fusion.3), channel_id=1, source_target_pairs={{0,16},{1,17},{2,18},{3,19},{4,20},{5,21},{6,22},{7,23},{8,24},{9,... | collective-permute-start | bytes 983048 | tf_op jit(solution)/shard_map/while/body/eval_jaxpr/ppermute | solution.py:12
  77.1 8.7 %copy-start.4 = (bf16[1,5120,2]{1,2,0:T(2,128)(2,1)S(1)}, bf16[1,5120,2]{1,2,0:T(2,128)(2,1)}, u32[]{:S(2)}) copy-start(bf16[1,5120,2]{1,2,0:T(2,128)(2,1)} %get-tuple-element.583) | copy-start | bytes 61444 | tf_op jit(solution)/shard_map/while
  80.1 14.7 %copy-start.2 = (bf16[1,32,5120]{2,1,0:T(8,128)(2,1)S(1)}, bf16[1,32,5120]{2,1,0:T(8,128)(2,1)}, u32[]{:S(2)}) copy-start(bf16[1,32,5120]{2,1,0:T(8,128)(2,1)} %get-tuple-element.564) | copy-start | bytes 983044 | tf_op jit(solution)/shard_map/while
  82.2 11.9 %all-to-all-start.1 = ((bf16[16,2,2560]{2,1,0:T(2,128)(2,1)}), bf16[16,2,2560]{2,1,0:T(2,128)(2,1)S(1)}, u32[]{:S(2)}, u32[]{:S(2)}) async-start(bf16[16,2,2560]{2,1,0:T(2,128)(2,1)} %reshape.191), calls=%async_computation.1 | async-start | bytes 327680 | tf_op jit(solution)/shard_map/while/body/eval_jaxpr/all_to_all | solution.py:68
  96.4 0.7 copy-start.3
